TPU v7x, 32 devices: a whole 2x2x4 slice. The times are simulated.
32 devices in a mesh: groups: 2 (over y), seq: 4 (over z), head: 4 (over x, core).
Axes of the slice: x: 2, y: 2, z: 4, core: 2. Of those that a mesh axis runs over, the one named last changes fastest.
Arguments:
- tile_rows: bfloat16 [8192, 1536], P(('groups', 'seq', 'head')), parts along dimension 0, may hold values from -6 to 6
- tile_route: int32 [8192, 2], P(('groups', 'seq', 'head')), parts along dimension 0, may hold values from 0 to 255, as said below
- embed_weight: bfloat16 [1536, 768], replicated, may hold values from -0.15625 to 0.15625
- norm_gain: float32 [768], replicated, may hold values from 0.1 to 1.9
- qkv_weight: bfloat16 [768, 16, 3, 48], P(None, 'head'), may hold values from -1 to 1
- out_weight: bfloat16 [768, 768], P('head'), may hold values from -0.21875 to 0.21875
Outputs:
- mixed: bfloat16 [8192, 768], P(('groups', 'seq', 'head')), parts along dimension 0
There are 2 independent parts, one for each index of `groups`. A program takes and returns all parts, laid end to end along the dimension named above; an argument that names none is the same for every part. Nothing has to cross between parts.
Inputs may be any that keep to these rules, and one draw needn't show every extreme that they name: `tile_route`: A tile's owner holds the same head class as the tile's own device. From one device at most 128 tiles go to one index of seq, and some device sends exactly 128 to one index in every draw; every slot of every owner receives exactly one tile.
All inputs are finite; a program needn't handle non-finite values.
Results may differ from a plain program's by a relative error of at most 0.0075.
Values may be sent and summed in bfloat16 or wider, within the bound.
A program may use at most 64 MiB of HBM per device.

v0:
```python
import jax
import jax.numpy as jnp
from jax import lax
from jax.sharding import PartitionSpec as P

EPSILON = 1e-05
DILATIONS = (1, 4, 16)
FRACTIONS = (16, 4, 1)


def from_partner(block, axis, apart):
    count = lax.axis_size(axis)
    route = []
    for low in range(count):
        high = low | 1 << apart
        if high != low and high < count:
            route += [(low, high), (high, low)]
    return lax.ppermute(block, axis, route)


def layer_norm(rows, gain):
    row_mean = jnp.mean(rows, axis=-1, keepdims=True)
    centered = rows - row_mean
    row_var = jnp.mean(centered * centered, axis=-1, keepdims=True)
    return (centered * lax.rsqrt(row_var + EPSILON) * gain).astype(jnp.bfloat16)


def attend_block(queries, key_rows, values):
    score_scale = queries.shape[-1] ** (-0.5)
    scores = jnp.dot(queries, key_rows.T, preferred_element_type=jnp.float32) * score_scale
    row_max = jnp.max(scores, axis=-1)
    expo = jnp.exp(scores - row_max[:, None])
    denominator = jnp.sum(expo, axis=-1)
    weights = (expo / denominator[:, None]).astype(jnp.bfloat16)
    head_out = jnp.dot(weights, values, preferred_element_type=jnp.float32)
    return (head_out, row_max + jnp.log(denominator))


def attend(queries, key_rows, values):
    count = queries.shape[0]
    if count > 512 and count % 512 == 0:
        blocks = queries.reshape(count // 512, 512, queries.shape[1])
        head_out, log_total = lax.map(
            lambda block_in: attend_block(block_in, key_rows, values), blocks
        )
        return (head_out.reshape(count, -1), log_total.reshape(count))
    return attend_block(queries, key_rows, values)


def expand_rows(head_out, log_total, offset, dilation):
    count = head_out.shape[0]
    pick_mask = jnp.arange(dilation, dtype=jnp.int32) == offset
    full_out = jnp.where(pick_mask[None, :, None], head_out[:, None, :], 0.0).reshape(
        count * dilation, -1
    )
    full_total = jnp.where(pick_mask[None, :], log_total[:, None], -1e30).reshape(count * dilation)
    return (full_out, full_total)


def merge_scales(outputs, totals):
    row_max = jnp.maximum(jnp.maximum(totals[0], totals[1]), totals[2])
    numer = jnp.zeros_like(outputs[0])
    denom = jnp.zeros_like(totals[0])
    for full_out, full_total in zip(outputs, totals):
        factor = jnp.exp(full_total - row_max)
        numer = numer + factor[:, None] * full_out
        denom = denom + factor
    return numer / denom[:, None]


def collect_segment(flat_rows, levels, seq_index):
    for level in range(levels):
        partner = from_partner(flat_rows, "seq", level)
        upper_half = seq_index >> level & 1 == 1
        lower_rows = jnp.where(upper_half, partner, flat_rows)
        upper_rows = jnp.where(upper_half, flat_rows, partner)
        flat_rows = jnp.concatenate([lower_rows, upper_rows], axis=0)
    return flat_rows


def local(tile_rows, tile_route, embed_weight, norm_gain, qkv_weight, out_weight):
    seq_count = lax.axis_size("seq")
    seq_index = lax.axis_index("seq")
    in_rows = tile_rows.shape[0]
    width = embed_weight.shape[1]
    capacity = 2 * in_rows // seq_count
    projected = jnp.dot(tile_rows, embed_weight, preferred_element_type=jnp.float32).astype(
        jnp.bfloat16
    )
    dest_seq = tile_route[:, 0]
    slot_index = tile_route[:, 1]
    owner_hits = (dest_seq[:, None] == jnp.arange(seq_count, dtype=jnp.int32)[None, :]).astype(
        jnp.int32
    )
    earlier = jnp.cumsum(owner_hits, axis=0) - owner_hits
    owner_rank = jnp.sum(earlier * owner_hits, axis=1)
    buffer_place = dest_seq * capacity + owner_rank
    send_pick = jnp.arange(seq_count * capacity, dtype=jnp.int32)[:, None] == buffer_place[None, :]
    outgoing = jnp.dot(
        send_pick.astype(jnp.bfloat16), projected, preferred_element_type=jnp.float32
    ).astype(jnp.bfloat16)
    outgoing_slot = jnp.sum(jnp.where(send_pick, slot_index[None, :] + 1, 0), axis=1)
    arrived, arrived_slot = (
        lax.all_to_all(
            outgoing.reshape(seq_count, capacity, width),
            "seq",
            split_axis=0,
            concat_axis=0,
            tiled=True,
        ),
        lax.all_to_all(
            outgoing_slot.reshape(seq_count, capacity),
            "seq",
            split_axis=0,
            concat_axis=0,
            tiled=True,
        ),
    )
    landing = jnp.arange(in_rows, dtype=jnp.int32)[:, None] + 1 == arrived_slot.reshape(-1)[None, :]
    embedded = jnp.dot(
        landing.astype(jnp.bfloat16), arrived.reshape(-1, width), preferred_element_type=jnp.float32
    )
    normed = layer_norm(embedded, norm_gain)
    heads_here = qkv_weight.shape[1]
    head_dim = qkv_weight.shape[3]
    weight_flat = qkv_weight.reshape(width, -1)
    qkv = jnp.dot(
        lax.all_gather(normed, "head", axis=0, tiled=True),
        weight_flat,
        preferred_element_type=jnp.float32,
    ).astype(jnp.bfloat16)
    rows_here = qkv.shape[0]
    qkv = qkv.reshape(rows_here, heads_here, 3, head_dim)
    first_head = lax.axis_index("head") * heads_here
    total_rows = rows_here * seq_count
    outputs = [[] for member in range(heads_here)]
    totals = [[] for member in range(heads_here)]
    for fraction, dilation in zip(FRACTIONS, DILATIONS):
        segment = total_rows // fraction
        per_segment = segment // dilation
        count = rows_here // dilation
        shaped = qkv.reshape(count, dilation, heads_here, 3, head_dim)
        offsets = []
        chosen = []
        for member in range(heads_here):
            offset = (first_head + member) % dilation
            offsets.append(offset)
            chosen.append(
                lax.dynamic_index_in_dim(shaped[:, :, member], offset, axis=1, keepdims=False)
            )
        chosen = jnp.stack(chosen, axis=1)
        queries = chosen[:, :, 0]
        pairs = chosen[:, :, 1:]
        if segment > rows_here:
            levels = (segment // rows_here).bit_length() - 1
            flat_rows = collect_segment(pairs.reshape(count, -1), levels, seq_index)
            pairs = flat_rows.reshape(per_segment, heads_here, 2, head_dim)
            groups = 1
        else:
            groups = rows_here // segment
        grouped_queries = queries.reshape(groups, count // groups, heads_here, head_dim)
        grouped_pairs = pairs.reshape(groups, per_segment, heads_here, 2, head_dim)
        for member in range(heads_here):
            head_out, log_total = lax.map(
                lambda block_in: attend(block_in[0], block_in[1][:, 0], block_in[1][:, 1]),
                (grouped_queries[:, :, member], grouped_pairs[:, :, member]),
            )
            full_out, full_total = expand_rows(
                head_out.reshape(count, head_dim),
                log_total.reshape(count),
                offsets[member],
                dilation,
            )
            outputs[member].append(full_out)
            totals[member].append(full_total)
    merged = [
        merge_scales(outputs[member], totals[member]).astype(jnp.bfloat16)
        for member in range(heads_here)
    ]
    attention = jnp.stack(merged, axis=1).reshape(rows_here, heads_here * head_dim)
    regrouped = lax.all_to_all(attention, "head", split_axis=0, concat_axis=1, tiled=True)
    branch = jnp.dot(
        regrouped,
        lax.all_gather(out_weight, "head", axis=0, tiled=True),
        preferred_element_type=jnp.float32,
    )
    return (embedded + branch).astype(jnp.bfloat16)


def solution(mesh):
    return jax.shard_map(
        local,
        mesh=mesh,
        in_specs=(
            P(("groups", "seq", "head"), None),
            P(("groups", "seq", "head"), None),
            P(),
            P(),
            P(None, "head", None, None),
            P("head", None),
        ),
        out_specs=P(("groups", "seq", "head"), None),
        check_vma=False,
    )
```

profile of v0, /device:TPU:1, one launch (start us, length us, event | category | flops | bytes accessed | tf_op | source)
XLA Modules:
  0.0 300.9 jit_solution(2592736077684952324)
XLA Ops:
  9.8 5.4 %all-to-all-start = ((s32[4,1,128]{2,1,0:T(1,128)}), s32[4,1,128]{2,1,0:T(1,128)S(1)}, u32[]{:S(2)}, u32[]{:S(2)}) async-start(s32[4,1,128]{2,1,0:T(1,128)} %bitcast.29), calls=%async_computation | async-start | bytes 4096 | tf_op jit(solution)/shard_map/all_to_all | solution.py:111
  15.2 3.2 %convolution_convert_fusion.1 = bf16[512,768]{1,0:T(8,128)(2,1)} fusion(bf16[256,1536]{1,0:T(8,128)(2,1)} %param.14, bf16[1536,768]{1,0:T(8,128)(2,1)S(1)} %copy-done, s32[256]{0:T(256)S(1)} %multiply_add_fusion), kind=kOutput, calls=%fused_computation.49 | convolution fusion | flops 806027264 | bytes 3933184 | tf_op jit(solution)/shard_map/dot_general | solution.py:99
  19.5 3.5 %all-to-all-start.1 = ((bf16[4,128,768]{2,1,0:T(8,128)(2,1)}), bf16[4,128,768]{2,1,0:T(8,128)(2,1)S(1)}, u32[]{:S(2)}, u32[]{:S(2)}) async-start(bf16[4,128,768]{2,1,0:T(8,128)(2,1)} %bitcast.363), calls=%async_computation.1 | async-start | bytes 1572864 | tf_op jit(solution)/shard_map/all_to_all | solution.py:104
  23.1 19.6 %all-to-all-done.1 = bf16[4,128,768]{2,1,0:T(8,128)(2,1)S(1)} async-done(((bf16[4,128,768]{2,1,0:T(8,128)(2,1)}), bf16[4,128,768]{2,1,0:T(8,128)(2,1)S(1)}, u32[]{:S(2)}, u32[]{:S(2)}) %all-to-all-start.1) | async-done | bytes 786464 | tf_op jit(solution)/shard_map/all_to_all | solution.py:104
  53.0 13.4 %all-gather.3.cloned.1.call-done = bf16[1024,768]{1,0:T(8,128)(2,1)} async-done(((bf16[256,768]{1,0:T(8,128)(2,1)}), bf16[1024,768]{1,0:T(8,128)(2,1)}) %all-gather.3.cloned.1.call-update) | async-done | bytes 1572880 | tf_op jit(solution)/shard_map/all_gather | solution.py:128
  66.4 3.8 %convolution_convert_fusion = bf16[1024,576]{0,1:T(8,128)(2,1)} fusion(bf16[1024,768]{1,0:T(8,128)(2,1)} %all-gather.3.cloned.1.call-done, bf16[768,576]{0,1:T(8,128)(2,1)} %bitcast.399), kind=kOutput, calls=%fused_computation.48 | convolution fusion | flops 906559488 | bytes 3637248 | tf_op jit(solution)/shard_map/dot_general | solution.py:127
  70.1 2.5 copy.117
  72.6 10.5 %reshape_reshape.14 = bf16[64,16,4,3,48]{4,3,2,1,0:T(4,128)(2,1)} reshape(bf16[1024,576]{1,0:T(8,128)(2,1)} %copy.117) | data formatting | bytes 2359296 | tf_op jit(solution)/shard_map/reshape;reshape | solution.py:142
  83.1 10.5 %reshape_reshape.13 = bf16[256,4,4,3,48]{4,3,2,1,0:T(4,128)(2,1)} reshape(bf16[1024,576]{1,0:T(8,128)(2,1)} %copy.117) | data formatting | bytes 2359296 | tf_op jit(solution)/shard_map/reshape;reshape | solution.py:142
  93.7 4.0 %fusion.46 = (bf16[256,4,1,3,48]{4,3,2,1,0:T(4,128)(2,1)}, bf16[256,4,1,3,48]{4,3,2,1,0:T(4,128)(2,1)S(1)}, bf16[256,4,1,3,48]{4,3,2,1,0:T(4,128)(2,1)S(1)}, bf16[256,4,1,3,48]{4,3,2,1,0:T(4,128)(2,1)}) fusion(bf16[256,4,4,3,48]{4,3,2,1,0:T(4,128)(2,1)} %reshape_reshape.13), kind=kLoop, calls=%fused_computation.230 | loop fusion | bytes 2359296 | tf_op jit(solution)/shard_map/slice | solution.py:149
  113.2 2.9 fusion.47
  130.6 2.6 reshape.1464
  136.8 18.2 %while.11 = (s32[]{:T(128)}, f32[4,256,48]{1,0,2:T(4,128)}, f32[4,256]{1,0:T(4,128)S(1)}, bf16[4,256,48]{2,1,0:T(8,128)(2,1)}, bf16[4,256,2,48]{1,3,2,0:T(8,128)(2,1)}, /*index=5*/s32[]{:T(128)}, s32[]{:T(128)}) while((s32[]{:T(128)}, f32[4,256,48]{1,0,2:T(4,128)}, f32[4,256]{1,0:T(4,128)S(1)}, bf16[4,256,48]{2,1,0:T(8,128)(2,1)}, ...), condition=%wide.region_33.34_spmd, body=%wide.region_30.33_spmd.sunk | while | flops 13041410 | bytes 1255525 | solution.py:164
  157.3 18.2 %while.10 = (s32[]{:T(128)}, f32[4,256,48]{1,0,2:T(4,128)}, f32[4,256]{1,0:T(4,128)S(1)}, bf16[4,256,48]{2,1,0:T(8,128)(2,1)}, bf16[4,256,2,48]{1,3,2,0:T(8,128)(2,1)}, /*index=5*/s32[]{:T(128)}, s32[]{:T(128)}) while((s32[]{:T(128)}, f32[4,256,48]{1,0,2:T(4,128)}, f32[4,256]{1,0:T(4,128)S(1)}, bf16[4,256,48]{2,1,0:T(8,128)(2,1)}, ...), condition=%wide.region_25.26_spmd, body=%wide.region_22.25_spmd.sunk | while | flops 13041410 | bytes 1255525 | solution.py:164
  159.5 2.3 dynamic_update_slice.74
  164.1 2.3 dynamic_update_slice.74
  168.7 2.3 dynamic_update_slice.74
  173.2 2.3 dynamic_update_slice.74
  177.9 18.2 %while.9 = (s32[]{:T(128)}, f32[4,256,48]{1,0,2:T(4,128)}, f32[4,256]{1,0:T(4,128)S(1)}, bf16[4,256,48]{2,1,0:T(8,128)(2,1)}, bf16[4,256,2,48]{1,3,2,0:T(8,128)(2,1)}, /*index=5*/s32[]{:T(128)}, s32[]{:T(128)}) while((s32[]{:T(128)}, f32[4,256,48]{1,0,2:T(4,128)}, f32[4,256]{1,0:T(4,128)S(1)}, bf16[4,256,48]{2,1,0:T(8,128)(2,1)}, ...), condition=%wide.region_17.18_spmd, body=%wide.region_14.17_spmd.sunk | while | flops 13041410 | bytes 1255525 | solution.py:164
  180.1 2.3 dynamic_update_slice.72
  184.7 2.3 dynamic_update_slice.72
  189.2 2.3 dynamic_update_slice.72
  193.8 2.3 dynamic_update_slice.72
  199.5 15.1 %while.8 = (s32[]{:T(128)}, f32[4,256,48]{1,0,2:T(4,128)}, f32[4,256]{1,0:T(4,128)S(1)}, bf16[4,256,48]{2,1,0:T(8,128)(2,1)S(1)}, bf16[4,256,2,48]{1,3,2,0:T(8,128)(2,1)}, /*index=5*/s32[]{:T(128)}, s32[]{:T(128)}) while((s32[]{:T(128)}, f32[4,256,48]{1,0,2:T(4,128)}, f32[4,256]{1,0:T(4,128)S(1)}, bf16[4,256,48]{2,1,0:T(8,128)(2,1)S(1)}, ...), condition=%wide.region_9.10_spmd, body=%wide.region_6.9_spmd.sunk | while | flops 13041410 | bytes 1255525 | solution.py:164
  200.9 2.3 dynamic_update_slice.70
  204.6 2.3 dynamic_update_slice.70
  208.3 2.3 dynamic_update_slice.70
  212.0 2.3 dynamic_update_slice.70
  243.2 5.5 %collective-permute-done.1 = bf16[128,384]{0,1:T(8,128)(2,1)S(1)} collective-permute-done((bf16[128,384]{0,1:T(8,128)(2,1)S(1)}, bf16[128,384]{0,1:T(8,128)(2,1)S(1)}, u32[]{:S(2)}, u32[]{:S(2)}) %collective-permute-start.1) | collective-permute-done | bytes 98336 | tf_op jit(solution)/shard_map/ppermute | solution.py:18
  281.1 3.9 %all-to-all-start.2 = ((bf16[4,256,192]{1,2,0:T(8,128)(2,1)}), bf16[4,256,192]{1,2,0:T(8,128)(2,1)S(1)}, u32[]{:S(2)}, u32[]{:S(2)}) async-start(bf16[4,256,192]{1,2,0:T(8,128)(2,1)} %copy.150), calls=%async_computation.2 | async-start | bytes 786432 | tf_op jit(solution)/shard_map/all_to_all | solution.py:181
  285.0 6.4 %all-to-all-done.2 = bf16[4,256,192]{1,2,0:T(8,128)(2,1)S(1)} async-done(((bf16[4,256,192]{1,2,0:T(8,128)(2,1)}), bf16[4,256,192]{1,2,0:T(8,128)(2,1)S(1)}, u32[]{:S(2)}, u32[]{:S(2)}) %all-to-all-start.2) | async-done | bytes 393248 | tf_op jit(solution)/shard_map/all_to_all | solution.py:181
  291.5 2.5 fusion.16
  (350 shorter events, 158.3 us)
Async XLA Ops:
  6.5 8.7 %copy-start = (bf16[1536,768]{1,0:T(8,128)(2,1)S(1)}, bf16[1536,768]{1,0:T(8,128)(2,1)}, u32[]{:S(2)}) copy-start(bf16[1536,768]{1,0:T(8,128)(2,1)} %param.16) | copy-start | bytes 7077892
  9.8 9.8 %all-to-all-start = ((s32[4,1,128]{2,1,0:T(1,128)}), s32[4,1,128]{2,1,0:T(1,128)S(1)}, u32[]{:S(2)}, u32[]{:S(2)}) async-start(s32[4,1,128]{2,1,0:T(1,128)} %bitcast.29), calls=%async_computation | async-start | bytes 4096 | tf_op jit(solution)/shard_map/all_to_all | solution.py:111
  19.5 23.1 %all-to-all-start.1 = ((bf16[4,128,768]{2,1,0:T(8,128)(2,1)}), bf16[4,128,768]{2,1,0:T(8,128)(2,1)S(1)}, u32[]{:S(2)}, u32[]{:S(2)}) async-start(bf16[4,128,768]{2,1,0:T(8,128)(2,1)} %bitcast.363), calls=%async_computation.1 | async-start | bytes 1572864 | tf_op jit(solution)/shard_map/all_to_all | solution.py:104
  23.0 22.4 %copy-start.28 = (f32[768]{0:T(1024)S(1)}, f32[768]{0:T(1024)}, u32[]{:S(2)}) copy-start(f32[768]{0:T(1024)} %param.17) | copy-start | bytes 9220
  23.1 43.3 %all-gather.3.cloned.1.call-start = ((), (), s32[]{:S(2)}) async-start(), calls=%async_computation.3 | async-start | bytes 1966080 | tf_op jit(solution)/shard_map/all_gather | solution.py:128
  46.4 238.7 %all-gather.5.cloned.1.call-start = ((), (), s32[]{:S(2)}) async-start(), calls=%async_computation.4 | async-start | bytes 1474560 | tf_op jit(solution)/shard_map/all_gather | solution.py:184
  105.8 5.6 %copy-start.15 = (bf16[1,256,4,48]{1,3,2,0:T(8,128)(2,1)}, bf16[1,256,4,48]{1,3,2,0:T(8,128)(2,1)S(1)}, u32[]{:S(2)}) copy-start(bf16[1,256,4,48]{1,3,2,0:T(8,128)(2,1)S(1)} %maximum_bitcast_fusion) | copy-start | bytes 294916
  125.9 113.9 %collective-permute-start = (bf16[64,384]{0,1:T(8,128)(2,1)}, bf16[64,384]{0,1:T(8,128)(2,1)}, u32[]{:S(2)}, u32[]{:S(2)}) collective-permute-start(bf16[64,384]{0,1:T(8,128)(2,1)} %bitcast.57), channel_id=1, source_target_pairs={{0,4},{4,0},{8,12},{12,8},{1,5},{5,1},{9,13},{13,9},{2,6},{6,2},{1... | collective-permute-start | bytes 147464 | tf_op jit(solution)/shard_map/ppermute | solution.py:18
  177.9 18.2 %copy-start.20 = (bf16[256,2,48]{0,2,1:T(8,128)(2,1)S(1)}, bf16[256,2,48]{0,2,1:T(8,128)(2,1)}, u32[]{:S(2)}) copy-start(bf16[256,2,48]{0,2,1:T(8,128)(2,1)} %get-tuple-element.389) | copy-start | bytes 147460
  214.6 6.0 %copy-start.23 = (f32[4,256]{1,0:T(4,128)}, f32[4,256]{1,0:T(4,128)S(1)}, u32[]{:S(2)}) copy-start(f32[4,256]{1,0:T(4,128)S(1)} %get-tuple-element.230) | copy-start | bytes 12292
  215.2 10.0 %copy-start.5 = (f32[4,256,48]{1,0,2:T(4,128)S(1)}, f32[4,256,48]{1,0,2:T(4,128)}, u32[]{:S(2)}) copy-start(f32[4,256,48]{1,0,2:T(4,128)} %get-tuple-element.240) | copy-start | bytes 589828
  221.4 9.1 %copy-start.6 = (f32[4,256,48]{1,0,2:T(4,128)S(1)}, f32[4,256,48]{1,0,2:T(4,128)}, u32[]{:S(2)}) copy-start(f32[4,256,48]{1,0,2:T(4,128)} %get-tuple-element.233) | copy-start | bytes 589828
  226.7 10.9 %copy-start.4 = (f32[4,256,48]{1,0,2:T(4,128)S(1)}, f32[4,256,48]{1,0,2:T(4,128)}, u32[]{:S(2)}) copy-start(f32[4,256,48]{1,0,2:T(4,128)} %get-tuple-element.231) | copy-start | bytes 589828
  231.2 11.9 %copy-start.16 = (bf16[64,1,1,3,48]{0,4,3,2,1:T(8,128)(2,1)S(1)}, bf16[64,1,1,3,48]{0,4,3,2,1:T(8,128)(2,1)}, u32[]{:S(2)}) copy-start(bf16[64,1,1,3,48]{0,4,3,2,1:T(8,128)(2,1)} %copy.126) | copy-start | bytes 55300
  231.2 11.9 %copy-start.17 = (bf16[64,1,1,3,48]{0,4,3,2,1:T(8,128)(2,1)S(1)}, bf16[64,1,1,3,48]{0,4,3,2,1:T(8,128)(2,1)}, u32[]{:S(2)}) copy-start(bf16[64,1,1,3,48]{0,4,3,2,1:T(8,128)(2,1)} %copy.125) | copy-start | bytes 55300
  233.9 5.1 %copy-start.29 = (f32[256]{0:T(256)S(1)}, f32[256]{0:T(256)}, u32[]{:S(2)}) copy-start(f32[256]{0:T(256)} %log_add_fusion.7) | copy-start | bytes 3076
  233.9 9.2 %copy-start.18 = (bf16[64,1,1,3,48]{0,4,3,2,1:T(8,128)(2,1)S(1)}, bf16[64,1,1,3,48]{0,4,3,2,1:T(8,128)(2,1)}, u32[]{:S(2)}) copy-start(bf16[64,1,1,3,48]{0,4,3,2,1:T(8,128)(2,1)} %copy.124) | copy-start | bytes 55300
  233.9 9.2 %copy-start.19 = (bf16[64,1,1,3,48]{0,4,3,2,1:T(8,128)(2,1)S(1)}, bf16[64,1,1,3,48]{0,4,3,2,1:T(8,128)(2,1)}, u32[]{:S(2)}) copy-start(bf16[64,1,1,3,48]{0,4,3,2,1:T(8,128)(2,1)} %copy.123) | copy-start | bytes 55300
  240.9 7.8 %collective-permute-start.1 = (bf16[128,384]{0,1:T(8,128)(2,1)S(1)}, bf16[128,384]{0,1:T(8,128)(2,1)S(1)}, u32[]{:S(2)}, u32[]{:S(2)}) collective-permute-start(bf16[128,384]{0,1:T(8,128)(2,1)S(1)} %pad_maximum_fusion.12), channel_id=1, source_target_pairs={{0,8},{8,0},{4,12},{12,4},{1,9},{9,1},{5,13},{13,5},{2,10},{10,2},... | collective-permute-start | bytes 294920 | tf_op jit(solution)/shard_map/ppermute | solution.py:18
  259.6 14.1 %copy-start.21 = (f32[1024]{0:T(1024)S(1)}, f32[1024]{0:T(1024)}, u32[]{:S(2)}) copy-start(f32[1024]{0:T(1024)} %broadcast_in_dim.470) | copy-start | bytes 12292
  259.6 14.8 %copy-start.22 = (f32[1024]{0:T(1024)S(1)}, f32[1024]{0:T(1024)}, u32[]{:S(2)}) copy-start(f32[1024]{0:T(1024)} %broadcast_in_dim.454) | copy-start | bytes 12292
  259.6 15.5 %copy-start.7 = (f32[1024,1,48]{0,2,1:T(8,128)S(1)}, f32[1024,1,48]{0,2,1:T(8,128)}, u32[]{:S(2)}) copy-start(f32[1024,1,48]{0,2,1:T(8,128)} %broadcast_in_dim_reshape.23) | copy-start | bytes 589828
  261.2 15.0 %copy-start.8 = (f32[1024,1,48]{0,2,1:T(8,128)S(1)}, f32[1024,1,48]{0,2,1:T(8,128)}, u32[]{:S(2)}) copy-start(f32[1024,1,48]{0,2,1:T(8,128)} %broadcast_in_dim_reshape.21) | copy-start | bytes 589828
  272.1 5.2 %copy-start.9 = (f32[1024,1,48]{0,2,1:T(8,128)S(1)}, f32[1024,1,48]{0,2,1:T(8,128)}, u32[]{:S(2)}) copy-start(f32[1024,1,48]{0,2,1:T(8,128)} %broadcast_in_dim_reshape.19) | copy-start | bytes 589828
  272.1 5.2 %copy-start.11 = (f32[1024,1,48]{0,2,1:T(8,128)S(1)}, f32[1024,1,48]{0,2,1:T(8,128)}, u32[]{:S(2)}) copy-start(f32[1024,1,48]{0,2,1:T(8,128)} %copy.135) | copy-start | bytes 589828
  272.1 5.2 %copy-start.14 = (f32[1024,1,48]{0,2,1:T(8,128)S(1)}, f32[1024,1,48]{0,2,1:T(8,128)}, u32[]{:S(2)}) copy-start(f32[1024,1,48]{0,2,1:T(8,128)} %copy.137) | copy-start | bytes 589828
  272.1 6.0 %copy-start.10 = (f32[1024,1,48]{0,2,1:T(8,128)S(1)}, f32[1024,1,48]{0,2,1:T(8,128)}, u32[]{:S(2)}) copy-start(f32[1024,1,48]{0,2,1:T(8,128)} %broadcast_in_dim_reshape.17) | copy-start | bytes 589828
  272.2 6.0 %copy-start.12 = (f32[1024,1,48]{0,2,1:T(8,128)S(1)}, f32[1024,1,48]{0,2,1:T(8,128)}, u32[]{:S(2)}) copy-start(f32[1024,1,48]{0,2,1:T(8,128)} %copy.129) | copy-start | bytes 589828
  272.2 6.0 %copy-start.13 = (f32[1024,1,48]{0,2,1:T(8,128)S(1)}, f32[1024,1,48]{0,2,1:T(8,128)}, u32[]{:S(2)}) copy-start(f32[1024,1,48]{0,2,1:T(8,128)} %copy.131) | copy-start | bytes 589828
  272.2 6.0 %copy-start.26 = (pred[1024]{0:T(1024)(128)(4,1)S(1)}, pred[1024]{0:T(1024)(128)(4,1)}, u32[]{:S(2)}) copy-start(pred[1024]{0:T(1024)(128)(4,1)} %broadcast_in_dim.457) | copy-start | bytes 3076
  272.2 6.0 %copy-start.27 = (pred[1024]{0:T(1024)(128)(4,1)S(1)}, pred[1024]{0:T(1024)(128)(4,1)}, u32[]{:S(2)}) copy-start(pred[1024]{0:T(1024)(128)(4,1)} %broadcast_in_dim.452) | copy-start | bytes 3076
  281.1 10.4 %all-to-all-start.2 = ((bf16[4,256,192]{1,2,0:T(8,128)(2,1)}), bf16[4,256,192]{1,2,0:T(8,128)(2,1)S(1)}, u32[]{:S(2)}, u32[]{:S(2)}) async-start(bf16[4,256,192]{1,2,0:T(8,128)(2,1)} %copy.150), calls=%async_computation.2 | async-start | bytes 786432 | tf_op jit(solution)/shard_map/all_to_all | solution.py:181
  (5 other events, 14.8 us)
Sparse Core Ops, SparseCore 0:
  46.5 19.8 all-gather.2
  67.9 17.4 all-gather.4
where the time goes:
time: 306 us; the launch traced here: 301 us
  local copies, waits for them, and re-layouts  167 us (55%)
  waiting for transfers between devices  46.8 us (15%)
  matrix products  35.9 us (12%)
  other arithmetic  20.1 us (7%)
  starting transfers between devices  16.3 us (5%)
  between operations  14.1 us (5%)
    dynamic_update_slice x48, local copies, waits for them, and re-layouts, local(): lax.map(lambda block_in: attend(block_in[0], block_in[1][:, 0], block_in[...  38.2 us
    broadcast_in_dim x16, local copies, waits for them, and re-layouts, expand_rows(): jnp.where(pick_mask[None, :, None], head_out[:, None, :], 0.0)  26.5 us
    another operation x2, local copies, waits for them, and re-layouts, local(): shaped = qkv.reshape(count, dilation, heads_here, 3, head_dim)  21 us
    all_to_all x1, waiting for transfers between devices, local(): lax.all_to_all(outgoing.reshape(seq_count, capacity, width), 'seq', split...  19.6 us
    dot_general x24, matrix products, attend_block(): jnp.dot(queries, key_rows.T, preferred_element_type=jnp.float32)  17.1 us
    broadcast_in_dim x32, local copies, waits for them, and re-layouts, expand_rows(): jnp.where(pick_mask[None, :], log_total[:, None], -1e+30)  15.3 us
    dynamic_slice x12, local copies, waits for them, and re-layouts, local(): lax.dynamic_index_in_dim(shaped[:, :, member], offset, axis=1, keepdims=F...  15 us
    squeeze x18, local copies, waits for them, and re-layouts, local(): lax.map(lambda block_in: attend(block_in[0], block_in[1][:, 0], block_in[...  13.5 us
  transfers between devices with their start and end apart: 7, of which 5 were waited for; matrix products, arithmetic and copies ran while one was open for 71% of the time, Pallas kernels for 0%

commit v1 on v0

--- a/solution.py
+++ b/solution.py
@@ -1,6 +1,10 @@
+import functools
+
 import jax
 import jax.numpy as jnp
 from jax import lax
+from jax.experimental import pallas as pl
+from jax.experimental.pallas import tpu as pltpu
 from jax.sharding import PartitionSpec as P
 
 EPSILON = 1e-05
@@ -187,18 +191,465 @@
     return (embedded + branch).astype(jnp.bfloat16)
 
 
+MESH = pl.DeviceIdType.MESH
+LOWEST = -1e30
+
+
+def dot_nt(a, b):
+    return lax.dot_general(a, b, (((1,), (1,)), ((), ())), preferred_element_type=jnp.float32)
+
+
+def dot(a, b):
+    return jnp.dot(a, b, preferred_element_type=jnp.float32)
+
+
+def iota(shape, dim):
+    return lax.broadcasted_iota(jnp.int32, shape, dim)
+
+
+def layer_kernel(
+    dims,
+    tile_any,
+    route_ref,
+    embed_any,
+    gain_ref,
+    w_any,
+    wo_any,
+    out_ref,
+    tile_v,
+    embed_v,
+    wt,
+    wo_v,
+    outgoing,
+    arrived,
+    slot_out,
+    slot_in,
+    emb,
+    qs,
+    kvs,
+    kv2,
+    kx3,
+    kv3,
+    num,
+    top,
+    den,
+    load_sem,
+    local_sem,
+    w_send,
+    w_recv,
+    route_send,
+    route_recv,
+    slot_send,
+    slot_recv,
+    kv2_send,
+    kv2_recv,
+    kx3_send,
+    kx3_recv,
+    kv3_send,
+    kv3_recv,
+):
+    S, H, R, D, NC, M, E, SH, d2, d3 = dims
+    cap = arrived.shape[2]
+    cols = arrived.shape[3]
+    G = M * E
+    p2 = R // d2
+    p3 = R // d3
+    v_low = G // 128 * 128
+    VW = 2 * G - v_low
+    lead = G - v_low
+    scale = E ** (-0.5)
+    s = lax.axis_index("seq")
+    c = lax.axis_index("head")
+    near = c + 1 - 2 * (c % 2)
+    far = (c + 2) % H
+    near_far = (near + 2) % H
+    seq_to = [(s + k) % S for k in range(S)]
+    seq_from = [(s + S - k) % S for k in range(S)]
+
+    loads = [pltpu.make_async_copy(tile_any, tile_v, load_sem.at[0])]
+    for n in range(NC):
+        loads.append(
+            pltpu.make_async_copy(
+                embed_any.at[:, pl.ds(n * cols, cols)], embed_v.at[n], load_sem.at[1 + n]
+            )
+        )
+    for copy in loads:
+        copy.start()
+
+    barrier = pltpu.get_barrier_semaphore()
+    for k in range(1, S):
+        pl.semaphore_signal(barrier, inc=1, device_id={"seq": seq_to[k]}, device_id_type=MESH)
+    for peer in (near, far):
+        pl.semaphore_signal(barrier, inc=1, device_id={"head": peer}, device_id_type=MESH)
+
+    dest = route_ref[0:1, :]
+    slot = route_ref[1:2, :]
+    sub = max(8, S)
+    hits = iota((sub, R), 0) == dest
+    hits_f = jnp.where(hits, 1.0, 0.0)
+    below = jnp.where(iota((R, R), 0) < iota((R, R), 1), 1.0, 0.0).astype(jnp.bfloat16)
+    earlier = dot(hits_f.astype(jnp.bfloat16), below)
+    rank = jnp.sum(earlier * hits_f, axis=0, keepdims=True).astype(jnp.int32)
+    place = dest * cap + rank
+    pick = jnp.where(iota((S * cap, R), 0) == place, 1.0, 0.0).astype(jnp.bfloat16)
+    slot_f = jnp.broadcast_to((slot + 1).astype(jnp.float32), (8, R)).astype(jnp.bfloat16)
+    slot_rows = dot_nt(slot_f, pick).astype(jnp.int32)
+    for t in range(S):
+        slot_out[t] = slot_rows[:, t * cap : (t + 1) * cap]
+
+    pl.semaphore_wait(barrier, S - 1 + 2)
+
+    def remote(src, dst, send, recv, **device):
+        copy = pltpu.make_async_remote_copy(
+            src_ref=src,
+            dst_ref=dst,
+            send_sem=send,
+            recv_sem=recv,
+            device_id=device,
+            device_id_type=MESH,
+        )
+        return copy
+
+    slot_copies = []
+    for k in range(1, S):
+        copy = remote(
+            slot_out.at[seq_to[k]], slot_in.at[s], slot_send.at[k], slot_recv.at[k], seq=seq_to[k]
+        )
+        copy.start()
+        slot_copies.append(copy)
+    slot_in[s] = slot_out[s]
+
+    w_far, w_near, w_local = [], [], []
+    for x in range(4):
+        source = w_any.at[:, x] if x < 3 else wo_any
+        target = wt.at[c, x] if x < 3 else wo_v.at[c]
+        w_far.append(remote(source, target, w_send.at[0, x], w_recv.at[0, x], head=far))
+        w_near.append(remote(source, target, w_send.at[1, x], w_recv.at[1, x], head=near))
+        w_local.append(pltpu.make_async_copy(source, target, local_sem.at[x]))
+
+    def w_relay(x):
+        ref = wt.at[far, x] if x < 3 else wo_v.at[far]
+        return remote(ref, ref, w_send.at[2, x], w_recv.at[2, x], head=near)
+
+    for x in range(4):
+        w_far[x].start()
+    loads[0].wait()
+    route_copies = []
+    for n in range(NC):
+        loads[1 + n].wait()
+        projected = dot(tile_v[...], embed_v[n]).astype(jnp.bfloat16)
+        outgoing[n] = dot(pick, projected).astype(jnp.bfloat16).reshape(S, cap, cols)
+        row = []
+        for k in range(1, S):
+            copy = remote(
+                outgoing.at[n, seq_to[k]],
+                arrived.at[n, s],
+                route_send.at[n, k],
+                route_recv.at[n, k],
+                seq=seq_to[k],
+            )
+            copy.start()
+            row.append(copy)
+        route_copies.append(row)
+        arrived[n, s] = outgoing[n, s]
+    for x in range(4):
+        w_local[x].start()
+        w_near[x].start()
+
+    def original(position):
+        return (position % p3) * d3 + ((position // p3) % (d3 // d2)) * d2 + position // p2
+
+    for copy in slot_copies:
+        copy.wait_recv()
+    slots = jnp.concatenate([slot_in[t][0:1, :] for t in range(S)], axis=1)
+    landing = jnp.where(original(iota((R, S * cap), 0)) + 1 == slots, 1.0, 0.0).astype(jnp.bfloat16)
+    back = jnp.where(original(iota((R, R), 1)) == iota((R, R), 0), 1.0, 0.0).astype(jnp.bfloat16)
+
+    relays = [w_relay(x) for x in range(4)]
+    parts = []
+    for n in range(NC):
+        if n < 3:
+            w_far[n].wait_recv()
+            relays[n].start()
+        for copy in route_copies[n]:
+            copy.wait_recv()
+        parts.append(dot(landing, arrived[n].reshape(S * cap, cols)))
+    embedded = jnp.concatenate(parts, axis=1)
+    emb[...] = embedded.astype(jnp.bfloat16)
+    normed = layer_norm(embedded, gain_ref[...])
+
+    w_relay_in = [
+        remote(ref, ref, w_send.at[2, x], w_recv.at[2, x], head=near)
+        for x, ref in enumerate([wt.at[near_far, y] for y in range(3)] + [wo_v.at[near_far]])
+    ]
+    for x in (1, 2, 0):
+        w_local[x].wait()
+        w_near[x].wait_recv()
+        w_relay_in[x].wait_recv()
+    lane_head = (iota((p2, 2 * G), 1) % G) // E
+    for g in range(SH):
+        kv = dot_nt(normed, wt[g, 1:3].reshape(2 * G, D))
+        kvs[g] = kv.astype(jnp.bfloat16)
+        chosen = kv[0:p2]
+        for m in range(1, M):
+            chosen = jnp.where(lane_head == m, kv[m * p2 : (m + 1) * p2], chosen)
+        chosen = chosen.astype(jnp.bfloat16)
+        kv2[c, g] = chosen
+        kx3[g] = chosen[g * p3 : (g + 1) * p3]
+    kv2_far = remote(kv2.at[c], kv2.at[c], kv2_send.at[0], kv2_recv.at[0], head=far)
+    kv2_near = remote(kv2.at[c], kv2.at[c], kv2_send.at[1], kv2_recv.at[1], head=near)
+    kv2_relay = remote(kv2.at[far], kv2.at[far], kv2_send.at[2], kv2_recv.at[2], head=near)
+    kv2_relay_in = remote(
+        kv2.at[near_far], kv2.at[near_far], kv2_send.at[2], kv2_recv.at[2], head=near
+    )
+    kx3_copies = []
+    for k in range(1, S):
+        copy = remote(kx3, kv3.at[s, c], kx3_send.at[k], kx3_recv.at[k], seq=seq_to[k])
+        copy.start()
+        kx3_copies.append(copy)
+    kv2_far.start()
+    kv2_near.start()
+    for g in range(SH):
+        qs[g] = dot_nt(normed, wt[g, 0].reshape(G, D)).astype(jnp.bfloat16)
+
+    q_head = iota((R, G), 1) // E
+    v_head = (iota((R, VW), 1) - lead + 2 * E) // E - 2
+
+    def scale_one(g, carry):
+        queries = qs[g]
+        keys = kvs[g, :, 0:G]
+        values = kvs[g, :, v_low : 2 * G]
+        numer = jnp.zeros((R, VW), jnp.float32)
+        peak = jnp.zeros((R, VW), jnp.float32)
+        denom = jnp.ones((R, VW), jnp.float32)
+        for m in range(M):
+            mask = jnp.where(q_head == m, 1.0, 0.0).astype(jnp.bfloat16)
+            scores = dot_nt(queries * mask, keys)
+            row_max = jnp.max(scores, axis=-1, keepdims=True)
+            expo = jnp.exp((scores - row_max) * scale)
+            total = jnp.sum(expo, axis=-1, keepdims=True)
+            head_out = dot(expo.astype(jnp.bfloat16), values)
+            mine = v_head == m
+            numer = jnp.where(mine, head_out, numer)
+            peak = jnp.where(mine, row_max, peak)
+            denom = jnp.where(mine, total, denom)
+        num[g] = numer
+        top[g] = peak
+        den[g] = denom
+        return carry
+
+    lax.fori_loop(0, SH - 1, scale_one, 0)
+    w_far[3].wait_recv()
+    relays[3].start()
+    kv2_far.wait_recv()
+    kv2_relay.start()
+    kv3_far, kv3_near, kv3_relay, kv3_relay_in = [], [], [], []
+    for k in range(1, S):
+        kx3_copies[k - 1].wait_recv()
+        block = kv3.at[seq_from[k], c]
+        kv3_far.append(remote(block, block, kv3_send.at[0, k], kv3_recv.at[0, k], head=far))
+        kv3_near.append(remote(block, block, kv3_send.at[1, k], kv3_recv.at[1, k], head=near))
+        kv3_far[-1].start()
+        kv3_near[-1].start()
+        block = kv3.at[seq_from[k], far]
+        kv3_relay.append(remote(block, block, kv3_send.at[2, k], kv3_recv.at[2, k], head=near))
+        block = kv3.at[seq_from[k], near_far]
+        kv3_relay_in.append(remote(block, block, kv3_send.at[2, k], kv3_recv.at[2, k], head=near))
+    lax.fori_loop(SH - 1, SH, scale_one, 0)
+
+    kv2_near.wait_recv()
+    kv2_relay_in.wait_recv()
+
+    def merge(g, rows, mine, row_max, total, head_out):
+        old = top[g, rows, :]
+        this = jnp.where(mine, row_max, LOWEST)
+        peak = jnp.maximum(old, this)
+        keep = jnp.exp((old - peak) * scale)
+        add = jnp.where(mine, jnp.exp((this - peak) * scale), 0.0)
+        top[g, rows, :] = peak
+        num[g, rows, :] = num[g, rows, :] * keep + head_out * add
+        den[g, rows, :] = den[g, rows, :] * keep + total * add
+
+    q_diag = jnp.where(q_head == iota((R, G), 0) // p2, 1.0, 0.0).astype(jnp.bfloat16)
+    v_diag = v_head == iota((R, VW), 0) // p2
+
+    def scale_two(g, carry):
+        keys = kv2[:, g, :, 0:G].reshape(H * p2, G)
+        values = kv2[:, g, :, v_low : 2 * G].reshape(H * p2, VW)
+        scores = dot_nt(qs[g] * q_diag, keys)
+        row_max = jnp.max(scores, axis=-1, keepdims=True)
+        expo = jnp.exp((scores - row_max) * scale)
+        total = jnp.sum(expo, axis=-1, keepdims=True)
+        head_out = dot(expo.astype(jnp.bfloat16), values)
+        merge(g, pl.ds(0, R), v_diag, row_max, total, head_out)
+        return carry
+
+    lax.fori_loop(0, SH, scale_two, 0)
+    for k in range(1, S):
+        kv3_far[k - 1].wait_recv()
+        kv3_relay[k - 1].start()
+    for g in range(SH):
+        for other in range(H):
+            kv3[s, other, g] = kv2[other, g, g * p3 : (g + 1) * p3, :]
+    residual = dot(back, emb[...])
+    for k in range(1, S):
+        kv3_near[k - 1].wait_recv()
+        kv3_relay_in[k - 1].wait_recv()
+
+    q_small = jnp.where(
+        iota((M * p3, G), 1) // E == iota((M * p3, G), 0) // p3, 1.0, 0.0
+    ).astype(jnp.bfloat16)
+
+    def scale_three(g, carry):
+        starts = [pl.multiple_of(m * p2 + g * p3, p3) for m in range(M)]
+        queries = jnp.concatenate([qs[g, pl.ds(start, p3), :] for start in starts], axis=0)
+        keys = kv3[:, :, g, :, 0:G].reshape(S * H * p3, G)
+        values = kv3[:, :, g, :, v_low : 2 * G].reshape(S * H * p3, VW)
+        scores = dot_nt(queries * q_small, keys)
+        row_max = jnp.max(scores, axis=-1, keepdims=True)
+        expo = jnp.exp((scores - row_max) * scale)
+        total = jnp.sum(expo, axis=-1, keepdims=True)
+        head_out = dot(expo.astype(jnp.bfloat16), values)
+        for m in range(M):
+            part = slice(m * p3, (m + 1) * p3)
+            merge(
+                g,
+                pl.ds(starts[m], p3),
+                (iota((p3, VW), 1) >= lead + m * E) & (iota((p3, VW), 1) < lead + (m + 1) * E),
+                row_max[part],
+                total[part],
+                head_out[part],
+            )
+        return carry
+
+    lax.fori_loop(0, SH, scale_three, 0)
+
+    w_local[3].wait()
+    w_near[3].wait_recv()
+    w_relay_in[3].wait_recv()
+    mixed = residual
+    for g in range(SH):
+        attention = (num[g] / den[g]).astype(jnp.bfloat16)
+        ordered = dot(back, attention)[:, lead:VW].astype(jnp.bfloat16)
+        mixed = mixed + dot(ordered, wo_v[g])
+    out_ref[...] = mixed.astype(jnp.bfloat16)
+
+    sent = slot_copies + w_far + w_near + relays + [kv2_far, kv2_near, kv2_relay] + kx3_copies
+    sent += kv3_far + kv3_near + kv3_relay
+    for row in route_copies:
+        sent += row
+    for copy in sent:
+        copy.wait_send()
+
+
+def fused(tile_rows, tile_route, embed_weight, norm_gain, qkv_weight, out_weight):
+    S = lax.axis_size("seq")
+    H = lax.axis_size("head")
+    R, d_in = tile_rows.shape
+    D = embed_weight.shape[1]
+    M, E = qkv_weight.shape[1], qkv_weight.shape[3]
+    G = M * E
+    cap = 2 * R // S
+    NC = D // 256
+    SH = H
+    d2, d3 = DILATIONS[1:]
+    p2, p3 = R // d2, R // d3
+    VW = 2 * G - G // 128 * 128
+    bf, f32 = jnp.bfloat16, jnp.float32
+    any_spec = pl.BlockSpec(memory_space=pl.ANY)
+    vmem = pl.BlockSpec(memory_space=pltpu.VMEM)
+    dma = pltpu.SemaphoreType.DMA
+    return pl.pallas_call(
+        functools.partial(layer_kernel, (S, H, R, D, NC, M, E, SH, d2, d3)),
+        out_shape=jax.ShapeDtypeStruct((R, D), bf),
+        in_specs=[any_spec, vmem, any_spec, vmem, any_spec, any_spec],
+        out_specs=vmem,
+        scratch_shapes=[
+            pltpu.VMEM((R, d_in), bf),
+            pltpu.VMEM((NC, d_in, 256), bf),
+            pltpu.VMEM((H, 3, M, E, D), bf),
+            pltpu.VMEM((H, G, D), bf),
+            pltpu.VMEM((NC, S, cap, 256), bf),
+            pltpu.VMEM((NC, S, cap, 256), bf),
+            pltpu.VMEM((S, 8, cap), jnp.int32),
+            pltpu.VMEM((S, 8, cap), jnp.int32),
+            pltpu.VMEM((R, D), bf),
+            pltpu.VMEM((SH, R, G), bf),
+            pltpu.VMEM((SH, R, 2 * G), bf),
+            pltpu.VMEM((H, SH, p2, 2 * G), bf),
+            pltpu.VMEM((SH, p3, 2 * G), bf),
+            pltpu.VMEM((S, H, SH, p3, 2 * G), bf),
+            pltpu.VMEM((SH, R, VW), f32),
+            pltpu.VMEM((SH, R, VW), f32),
+            pltpu.VMEM((SH, R, VW), f32),
+            dma((1 + NC,)),
+            dma((4,)),
+            dma((3, 4)),
+            dma((3, 4)),
+            dma((NC, S)),
+            dma((NC, S)),
+            dma((S,)),
+            dma((S,)),
+            dma((3,)),
+            dma((3,)),
+            dma((S,)),
+            dma((S,)),
+            dma((3, S)),
+            dma((3, S)),
+        ],
+        compiler_params=pltpu.CompilerParams(
+            collective_id=0, has_side_effects=True, vmem_limit_bytes=56 * 1024 * 1024
+        ),
+    )(
+        tile_rows,
+        tile_route.T,
+        embed_weight,
+        norm_gain.reshape(1, D),
+        qkv_weight.transpose(1, 2, 3, 0),
+        out_weight,
+    )
+
+
+def fits(mesh):
+    def check(tile_rows, embed_weight, qkv_weight):
+        S, H = mesh.shape["seq"], mesh.shape["head"]
+        rows = tile_rows.shape[0] // mesh.size
+        heads = qkv_weight.shape[1] // H
+        d2, d3 = DILATIONS[1:]
+        return (
+            H == 4
+            and heads == d2
+            and heads * H == d3
+            and FRACTIONS[0] == S * H
+            and FRACTIONS[1] == S
+            and FRACTIONS[2] == 1
+            and rows % (16 * d3) == 0
+            and rows <= 256
+            and embed_weight.shape[1] % 256 == 0
+            and embed_weight.shape[1] // 256 >= 3
+        )
+
+    return check
+
+
 def solution(mesh):
-    return jax.shard_map(
-        local,
-        mesh=mesh,
-        in_specs=(
-            P(("groups", "seq", "head"), None),
-            P(("groups", "seq", "head"), None),
-            P(),
-            P(),
-            P(None, "head", None, None),
-            P("head", None),
-        ),
-        out_specs=P(("groups", "seq", "head"), None),
-        check_vma=False,
-    )
+    check = fits(mesh)
+
+    def program(tile_rows, tile_route, embed_weight, norm_gain, qkv_weight, out_weight):
+        body = fused if check(tile_rows, embed_weight, qkv_weight) else local
+        return jax.shard_map(
+            body,
+            mesh=mesh,
+            in_specs=(
+                P(("groups", "seq", "head"), None),
+                P(("groups", "seq", "head"), None),
+                P(),
+                P(),
+                P(None, "head", None, None),
+                P("head", None),
+            ),
+            out_specs=P(("groups", "seq", "head"), None),
+            check_vma=False,
+        )(tile_rows, tile_route, embed_weight, norm_gain, qkv_weight, out_weight)
+
+    return program

time: 306 us -> 50.6 us (0.17); the launches traced: 301 us -> 50.4 us
  local copies, waits for them, and re-layouts: 167 us -> 3.03 us
  Pallas kernels: 0 us -> 47.3 us
  waiting for transfers between devices: 46.8 us -> 0 us
  matrix products: 35.9 us -> 0 us
  other arithmetic: 20.1 us -> 0 us
  starting transfers between devices: 16.3 us -> 0 us
  between operations: 14.1 us -> 0.01 us
    pallas_call x0 -> x1, Pallas kernels: none -> 47.3 us  [fused(): pl.pallas_call(functools.partial(layer_kernel, (S, H, R, D, NC, M, E, SH,...]
    broadcast_in_dim x48 -> x0, local copies, waits for them, and re-layouts: 41.8 us -> none  [the longest x16 26.5 us: expand_rows(): jnp.where(pick_mask[None, :, None], head_out[:, None, :], 0.0)]
    dynamic_update_slice x48 -> x0, local copies, waits for them, and re-layouts: 38.2 us -> none  [local(): lax.map(lambda block_in: attend(block_in[0], block_in[1][:, 0], block_in[...]
    dot_general x52 -> x0, matrix products: 35.9 us -> none  [the longest x24 17.1 us: attend_block(): jnp.dot(queries, key_rows.T, preferred_element_type=jnp.float32)]
    another operation x18 -> x0, local copies, waits for them, and re-layouts: 28.1 us -> none  [the longest x2 21 us: local(): shaped = qkv.reshape(count, dilation, heads_here, 3, head_dim)]
    all_to_all x3 -> x0, waiting for transfers between devices: 27.1 us -> none  [the longest x1 19.6 us: local(): lax.all_to_all(outgoing.reshape(seq_count, capacity, width), 'seq', split...]
    squeeze x21 -> x0, local copies, waits for them, and re-layouts: 19.3 us -> none  [the longest x18 13.5 us: local(): lax.map(lambda block_in: attend(block_in[0], block_in[1][:, 0], block_in[...]
    dynamic_slice x12 -> x0, local copies, waits for them, and re-layouts: 15 us -> none  [local(): lax.dynamic_index_in_dim(shaped[:, :, member], offset, axis=1, keepdims=F...]
  transfers between devices with their start and end apart: 7 -> 0, of which waited for: 5 -> 0; matrix products, arithmetic and copies ran while one was open for 71% -> 0% of each run, Pallas kernels for 0% -> 0%
where the time goes in v1:
time: 50.6 us; the launch traced here: 50.4 us
  Pallas kernels  47.3 us (93%)
  local copies, waits for them, and re-layouts  3.03 us (6%)
    pallas_call x1, Pallas kernels, fused(): pl.pallas_call(functools.partial(layer_kernel, (S, H, R, D, NC, M, E, SH,...  47.3 us
    unnamed x1, local copies, waits for them, and re-layouts  1.77 us
    reshape x1, local copies, waits for them, and re-layouts, fused(): norm_gain.reshape(1, D)  1.27 us

profile of v1, /device:TPU:1, one launch (start us, length us, event | category | flops | bytes accessed | tf_op | source)
XLA Modules:
  0.0 50.4 jit_solution(17508929988346018498)
XLA Ops:
  0.0 1.3 %reshape.3.gain_ref = f32[1,768]{1,0:T(1,128)} reshape(f32[768]{0:T(1024)} %param.9) | data formatting | bytes 6144 | tf_op jit(solution)/shard_map/reshape | solution.py:607
  1.3 47.3 %shard_map.64 = bf16[256,768]{1,0:T(8,128)(2,1)} custom-call(bf16[256,1536]{1,0:T(8,128)(2,1)} %tile_any.1, s32[2,256]{1,0:T(2,128)} %bitcast.3, bf16[1536,768]{1,0:T(8,128)(2,1)} %embed_any.1, f32[1,768]{1,0:T(1,128)} %reshape.3.gain_ref, bf16[4,3,48,768]{3,2,1,0:T(8,128)(2,1)} %bitcast.2, bf16[192,768]{1,0:T(8,128)(2,1)} %wo_any.1), custom_call_target="tpu_custom_call" | custom-call | tf_op jit(solution)/shard_map/pallas_call | solution.py:562
  48.6 1.8 %copy.8 = bf16[256,768]{1,0:T(8,128)(2,1)} copy(bf16[256,768]{1,0:T(8,128)(2,1)} %shard_map.64) | data formatting | bytes 786432

commit v2 on v1

--- a/solution.py
+++ b/solution.py
@@ -260,6 +260,8 @@
     scale = E ** (-0.5)
     s = lax.axis_index("seq")
     c = lax.axis_index("head")
+    side = lax.axis_index("groups")
+    across = 1 - side
     near = c + 1 - 2 * (c % 2)
     far = (c + 2) % H
     near_far = (near + 2) % H
@@ -281,6 +283,7 @@
         pl.semaphore_signal(barrier, inc=1, device_id={"seq": seq_to[k]}, device_id_type=MESH)
     for peer in (near, far):
         pl.semaphore_signal(barrier, inc=1, device_id={"head": peer}, device_id_type=MESH)
+    pl.semaphore_signal(barrier, inc=1, device_id={"groups": across}, device_id_type=MESH)
 
     dest = route_ref[0:1, :]
     slot = route_ref[1:2, :]
@@ -297,7 +300,7 @@
     for t in range(S):
         slot_out[t] = slot_rows[:, t * cap : (t + 1) * cap]
 
-    pl.semaphore_wait(barrier, S - 1 + 2)
+    pl.semaphore_wait(barrier, S - 1 + 3)
 
     def remote(src, dst, send, recv, **device):
         copy = pltpu.make_async_remote_copy(
@@ -319,19 +322,57 @@
         slot_copies.append(copy)
     slot_in[s] = slot_out[s]
 
-    w_far, w_near, w_local = [], [], []
+    half_m, half_g = M // 2, G // 2
+
+    def w_block(owner, x):
+        return wt.at[owner, x] if x < 3 else wo_v.at[owner]
+
+    def w_half(owner, x, part):
+        if x < 3:
+            return wt.at[owner, x, pl.ds(part * half_m, half_m)]
+        return wo_v.at[owner, pl.ds(pl.multiple_of(part * half_g, half_g), half_g)]
+
+    def w_copy(source, target, stage, x, **device):
+        return remote(source, target, w_send.at[stage, x], w_recv.at[stage, x], **device)
+
+    w_far, w_near, w_local, w_over, w_pass, w_rest = [], [], [], [], [], []
+    w_over_in, w_pass_in, w_rest_in = [], [], []
     for x in range(4):
-        source = w_any.at[:, x] if x < 3 else wo_any
-        target = wt.at[c, x] if x < 3 else wo_v.at[c]
-        w_far.append(remote(source, target, w_send.at[0, x], w_recv.at[0, x], head=far))
-        w_near.append(remote(source, target, w_send.at[1, x], w_recv.at[1, x], head=near))
-        w_local.append(pltpu.make_async_copy(source, target, local_sem.at[x]))
-
-    def w_relay(x):
-        ref = wt.at[far, x] if x < 3 else wo_v.at[far]
-        return remote(ref, ref, w_send.at[2, x], w_recv.at[2, x], head=near)
-
-    for x in range(4):
+        if x < 3:
+            own, own_half = w_any.at[:, x], w_any.at[pl.ds(side * half_m, half_m), x]
+        else:
+            own = wo_any
+            own_half = wo_any.at[pl.ds(pl.multiple_of(side * half_g, half_g), half_g)]
+        w_far.append(w_copy(own_half, w_half(c, x, side), 0, x, head=far))
+        w_near.append(w_copy(own, w_block(c, x), 1, x, head=near))
+        w_local.append(pltpu.make_async_copy(own, w_block(c, x), local_sem.at[x]))
+        ref = w_half(far, x, side)
+        w_over.append(w_copy(ref, ref, 2, x, groups=across))
+        w_pass.append(w_copy(ref, ref, 3, x, head=near))
+        ref = w_half(far, x, across)
+        w_over_in.append(w_copy(ref, ref, 2, x, groups=across))
+        w_rest.append(w_copy(ref, ref, 4, x, head=near))
+        ref = w_half(near_far, x, side)
+        w_pass_in.append(w_copy(ref, ref, 3, x, head=near))
+        ref = w_half(near_far, x, across)
+        w_rest_in.append(w_copy(ref, ref, 4, x, head=near))
+
+    def w_first(x):
+        w_far[x].wait_recv()
+        w_over[x].start()
+        w_pass[x].start()
+
+    def w_second(x):
+        w_over_in[x].wait_recv()
+        w_rest[x].start()
+
+    def w_ready(x):
+        w_local[x].wait()
+        w_near[x].wait_recv()
+        w_pass_in[x].wait_recv()
+        w_rest_in[x].wait_recv()
+
+    for x in (1, 2, 0, 3):
         w_far[x].start()
     loads[0].wait()
     route_copies = []
@@ -352,7 +393,7 @@
             row.append(copy)
         route_copies.append(row)
         arrived[n, s] = outgoing[n, s]
-    for x in range(4):
+    for x in (1, 2, 0, 3):
         w_local[x].start()
         w_near[x].start()
 
@@ -365,12 +406,15 @@
     landing = jnp.where(original(iota((R, S * cap), 0)) + 1 == slots, 1.0, 0.0).astype(jnp.bfloat16)
     back = jnp.where(original(iota((R, R), 1)) == iota((R, R), 0), 1.0, 0.0).astype(jnp.bfloat16)
 
-    relays = [w_relay(x) for x in range(4)]
+    w_first(1)
+    w_first(2)
+    w_second(1)
+    w_first(0)
+    w_second(2)
+    w_first(3)
+    w_second(0)
     parts = []
     for n in range(NC):
-        if n < 3:
-            w_far[n].wait_recv()
-            relays[n].start()
         for copy in route_copies[n]:
             copy.wait_recv()
         parts.append(dot(landing, arrived[n].reshape(S * cap, cols)))
@@ -378,14 +422,8 @@
     emb[...] = embedded.astype(jnp.bfloat16)
     normed = layer_norm(embedded, gain_ref[...])
 
-    w_relay_in = [
-        remote(ref, ref, w_send.at[2, x], w_recv.at[2, x], head=near)
-        for x, ref in enumerate([wt.at[near_far, y] for y in range(3)] + [wo_v.at[near_far]])
-    ]
-    for x in (1, 2, 0):
-        w_local[x].wait()
-        w_near[x].wait_recv()
-        w_relay_in[x].wait_recv()
+    w_ready(1)
+    w_ready(2)
     lane_head = (iota((p2, 2 * G), 1) % G) // E
     for g in range(SH):
         kv = dot_nt(normed, wt[g, 1:3].reshape(2 * G, D))
@@ -409,6 +447,8 @@
         kx3_copies.append(copy)
     kv2_far.start()
     kv2_near.start()
+    w_second(3)
+    w_ready(0)
     for g in range(SH):
         qs[g] = dot_nt(normed, wt[g, 0].reshape(G, D)).astype(jnp.bfloat16)
 
@@ -439,8 +479,6 @@
         return carry
 
     lax.fori_loop(0, SH - 1, scale_one, 0)
-    w_far[3].wait_recv()
-    relays[3].start()
     kv2_far.wait_recv()
     kv2_relay.start()
     kv3_far, kv3_near, kv3_relay, kv3_relay_in = [], [], [], []
@@ -524,9 +562,7 @@
 
     lax.fori_loop(0, SH, scale_three, 0)
 
-    w_local[3].wait()
-    w_near[3].wait_recv()
-    w_relay_in[3].wait_recv()
+    w_ready(3)
     mixed = residual
     for g in range(SH):
         attention = (num[g] / den[g]).astype(jnp.bfloat16)
@@ -534,7 +570,7 @@
         mixed = mixed + dot(ordered, wo_v[g])
     out_ref[...] = mixed.astype(jnp.bfloat16)
 
-    sent = slot_copies + w_far + w_near + relays + [kv2_far, kv2_near, kv2_relay] + kx3_copies
+    sent = slot_copies + w_far + w_near + w_over + w_pass + w_rest + [kv2_far, kv2_near, kv2_relay] + kx3_copies
     sent += kv3_far + kv3_near + kv3_relay
     for row in route_copies:
         sent += row
@@ -584,8 +620,8 @@
             pltpu.VMEM((SH, R, VW), f32),
             dma((1 + NC,)),
             dma((4,)),
-            dma((3, 4)),
-            dma((3, 4)),
+            dma((5, 4)),
+            dma((5, 4)),
             dma((NC, S)),
             dma((NC, S)),
             dma((S,)),
@@ -618,6 +654,7 @@
         d2, d3 = DILATIONS[1:]
         return (
             H == 4
+            and mesh.shape["groups"] == 2
             and heads == d2
             and heads * H == d3
             and FRACTIONS[0] == S * H

time: 50.6 us -> 44.5 us (0.88)
  Pallas kernels: 47.3 us -> 41.2 us
    pallas_call x1, Pallas kernels: 47.3 us -> 41.2 us  [fused(): pl.pallas_call(functools.partial(layer_kernel, (S, H, R, D, NC, M, E, SH,...]
where the time goes in v2:
time: 44.5 us; the launch traced here: 44.3 us
  Pallas kernels  41.2 us (93%)
  local copies, waits for them, and re-layouts  3.03 us (7%)
    pallas_call x1, Pallas kernels, fused(): pl.pallas_call(functools.partial(layer_kernel, (S, H, R, D, NC, M, E, SH,...  41.2 us
    unnamed x1, local copies, waits for them, and re-layouts  1.77 us
    reshape x1, local copies, waits for them, and re-layouts, fused(): norm_gain.reshape(1, D)  1.27 us

profile of v2, /device:TPU:1, one launch (start us, length us, event | category | flops | bytes accessed | tf_op | source)
XLA Modules:
  0.0 44.3 jit_solution(8802355911211650083)
XLA Ops:
  0.0 1.3 %reshape.3.gain_ref = f32[1,768]{1,0:T(1,128)} reshape(f32[768]{0:T(1024)} %param.9) | data formatting | bytes 6144 | tf_op jit(solution)/shard_map/reshape | solution.py:643
  1.3 41.2 %shard_map.64 = bf16[256,768]{1,0:T(8,128)(2,1)} custom-call(bf16[256,1536]{1,0:T(8,128)(2,1)} %tile_any.1, s32[2,256]{1,0:T(2,128)} %bitcast.3, bf16[1536,768]{1,0:T(8,128)(2,1)} %embed_any.1, f32[1,768]{1,0:T(1,128)} %reshape.3.gain_ref, bf16[4,3,48,768]{3,2,1,0:T(8,128)(2,1)} %bitcast.2, bf16[192,768]{1,0:T(8,128)(2,1)} %wo_any.1), custom_call_target="tpu_custom_call" | custom-call | tf_op jit(solution)/shard_map/pallas_call | solution.py:598
  42.5 1.8 %copy.8 = bf16[256,768]{1,0:T(8,128)(2,1)} copy(bf16[256,768]{1,0:T(8,128)(2,1)} %shard_map.64) | data formatting | bytes 786432

commit v3 on v2

--- a/solution.py
+++ b/solution.py
@@ -372,8 +372,6 @@
         w_pass_in[x].wait_recv()
         w_rest_in[x].wait_recv()
 
-    for x in (1, 2, 0, 3):
-        w_far[x].start()
     loads[0].wait()
     route_copies = []
     for n in range(NC):
@@ -392,6 +390,9 @@
             copy.start()
             row.append(copy)
         route_copies.append(row)
+        if n == 0:
+            for x in (1, 2, 0, 3):
+                w_far[x].start()
         arrived[n, s] = outgoing[n, s]
     for x in (1, 2, 0, 3):
         w_local[x].start()
@@ -411,7 +412,6 @@
     w_second(1)
     w_first(0)
     w_second(2)
-    w_first(3)
     w_second(0)
     parts = []
     for n in range(NC):
@@ -420,7 +420,7 @@
         parts.append(dot(landing, arrived[n].reshape(S * cap, cols)))
     embedded = jnp.concatenate(parts, axis=1)
     emb[...] = embedded.astype(jnp.bfloat16)
-    normed = layer_norm(embedded, gain_ref[...])
+    normed = layer_norm(embedded, gain_ref[...].reshape(1, D))
 
     w_ready(1)
     w_ready(2)
@@ -447,7 +447,7 @@
         kx3_copies.append(copy)
     kv2_far.start()
     kv2_near.start()
-    w_second(3)
+    w_first(3)
     w_ready(0)
     for g in range(SH):
         qs[g] = dot_nt(normed, wt[g, 0].reshape(G, D)).astype(jnp.bfloat16)
@@ -479,6 +479,7 @@
         return carry
 
     lax.fori_loop(0, SH - 1, scale_one, 0)
+    w_second(3)
     kv2_far.wait_recv()
     kv2_relay.start()
     kv3_far, kv3_near, kv3_relay, kv3_relay_in = [], [], [], []
@@ -640,7 +641,7 @@
         tile_rows,
         tile_route.T,
         embed_weight,
-        norm_gain.reshape(1, D),
+        norm_gain,
         qkv_weight.transpose(1, 2, 3, 0),
         out_weight,
     )

time: 44.5 us -> 43 us (0.966)
  local copies, waits for them, and re-layouts: 3.03 us -> 1.77 us
    reshape x1 -> x0, local copies, waits for them, and re-layouts: 1.27 us -> none  [fused(): norm_gain.reshape(1, D)]
where the time goes in v3:
time: 43 us; the launch traced here: 42.8 us
  Pallas kernels  41 us (95%)
  local copies, waits for them, and re-layouts  1.77 us (4%)
    pallas_call x1, Pallas kernels, fused(): pl.pallas_call(functools.partial(layer_kernel, (S, H, R, D, NC, M, E, SH,...  41 us
    unnamed x1, local copies, waits for them, and re-layouts  1.77 us

profile of v3, /device:TPU:1, one launch (start us, length us, event | category | flops | bytes accessed | tf_op | source)
XLA Modules:
  0.0 42.8 jit_solution(15360874152065496548)
XLA Ops:
  0.0 41.0 %shard_map.64 = bf16[256,768]{1,0:T(8,128)(2,1)} custom-call(bf16[256,1536]{1,0:T(8,128)(2,1)} %tile_any.1, s32[2,256]{1,0:T(2,128)} %bitcast.3, bf16[1536,768]{1,0:T(8,128)(2,1)} %embed_any.1, f32[768]{0:T(1024)} %gain_ref.1, bf16[4,3,48,768]{3,2,1,0:T(8,128)(2,1)} %bitcast.2, bf16[192,768]{1,0:T(8,128)(2,1)} %wo_any.1), custom_call_target="tpu_custom_call" | custom-call | tf_op jit(solution)/shard_map/pallas_call | solution.py:599
  41.0 1.8 %copy.8 = bf16[256,768]{1,0:T(8,128)(2,1)} copy(bf16[256,768]{1,0:T(8,128)(2,1)} %shard_map.64) | data formatting | bytes 786432

commit v4 on v3

--- a/solution.py
+++ b/solution.py
@@ -372,6 +372,8 @@
         w_pass_in[x].wait_recv()
         w_rest_in[x].wait_recv()
 
+    for x in (1, 2, 0, 3):
+        w_far[x].start()
     loads[0].wait()
     route_copies = []
     for n in range(NC):
@@ -390,9 +392,6 @@
             copy.start()
             row.append(copy)
         route_copies.append(row)
-        if n == 0:
-            for x in (1, 2, 0, 3):
-                w_far[x].start()
         arrived[n, s] = outgoing[n, s]
     for x in (1, 2, 0, 3):
         w_local[x].start()

time: 43 us -> 43 us (level)
  no operation moved by 1% of the time
where the time goes in v4:
time: 43 us; the launch traced here: 42.8 us
  Pallas kernels  41 us (95%)
  local copies, waits for them, and re-layouts  1.77 us (4%)
    pallas_call x1, Pallas kernels, fused(): pl.pallas_call(functools.partial(layer_kernel, (S, H, R, D, NC, M, E, SH,...  41 us
    unnamed x1, local copies, waits for them, and re-layouts  1.77 us

profile of v4, /device:TPU:1, one launch (start us, length us, event | category | flops | bytes accessed | tf_op | source)
XLA Modules:
  0.0 42.8 jit_solution(4410909550231838504)
XLA Ops:
  0.0 41.0 %shard_map.64 = bf16[256,768]{1,0:T(8,128)(2,1)} custom-call(bf16[256,1536]{1,0:T(8,128)(2,1)} %tile_any.1, s32[2,256]{1,0:T(2,128)} %bitcast.3, bf16[1536,768]{1,0:T(8,128)(2,1)} %embed_any.1, f32[768]{0:T(1024)} %gain_ref.1, bf16[4,3,48,768]{3,2,1,0:T(8,128)(2,1)} %bitcast.2, bf16[192,768]{1,0:T(8,128)(2,1)} %wo_any.1), custom_call_target="tpu_custom_call" | custom-call | tf_op jit(solution)/shard_map/pallas_call | solution.py:598
  41.0 1.8 %copy.8 = bf16[256,768]{1,0:T(8,128)(2,1)} copy(bf16[256,768]{1,0:T(8,128)(2,1)} %shard_map.64) | data formatting | bytes 786432
